TPU v7x, 32 devices: a whole 2x2x4 slice. The times are simulated.
32 devices in a mesh: grp: 4 (over x, core), tp: 4 (over z), cores: 2 (over y).
Axes of the slice: x: 2, y: 2, z: 4, core: 2. Of those that a mesh axis runs over, the one named last changes fastest.
Arguments:
- tokens: bfloat16 [4096, 8192], P('grp', ('tp', 'cores')), may hold values from -6 to 6
- gate_up_weight: bfloat16 [8192, 2, 16384], P(None, None, ('tp', 'cores')), may hold values from -0.0625 to 0.0625
- down_factor_pool: bfloat16 [8, 8192, 256], P(('tp', 'cores'), 'grp'), may hold values from -0.0625 to 0.0625
- up_factor_pool: bfloat16 [8, 4, 8, 128, 1024], P(('tp', 'cores'), 'grp'), may hold values from -0.5 to 0.5
- segment_adapters: int32 [4, 3], replicated, may hold values from 0 to 7
- segment_tile_counts: int32 [4, 3], P('grp'), may hold values from 1 to 4, 8 in all within a row
- adapter_pool_rows: int32 [8], replicated, may hold values from 0 to 7, each once
Outputs:
- hidden: bfloat16 [4096, 16384], P('grp', ('tp', 'cores'))
Inputs may be any that keep to these rules, and one draw needn't show every extreme that they name: `segment_tile_counts`: each row sums to 8. `adapter_pool_rows`: each pool row appears once.
All inputs are finite; a program needn't handle non-finite values.
Results may differ from a plain program's by a relative error of at most 0.0036.
Values may be sent and summed in bfloat16 or wider, within the bound.
A program may use at most 320 MiB of HBM per device.

v0:
```python
import jax
import jax.numpy as jnp
from jax import lax
from jax.sharding import PartitionSpec as P

TILE = 128
adapter_scale = 0.5


def tile_segments(tile_lengths, tile_count):
    bounds = jnp.cumsum(tile_lengths)
    positions = jnp.arange(tile_count, dtype=jnp.int32)
    return jnp.sum((bounds[None, :] <= positions[:, None]).astype(jnp.int32), axis=1)


def per_device(
    tokens,
    gate_up_weight,
    down_factor_pool,
    up_factor_pool,
    segment_adapters,
    segment_tile_counts,
    adapter_pool_rows,
):
    groups = lax.axis_size("grp")
    device_shares = lax.axis_size(("tp", "cores"))
    piece_index = lax.axis_index(("tp", "cores"))
    token_count = tokens.shape[0]
    full_width = tokens.shape[1] * device_shares
    local_hidden_width = gate_up_weight.shape[2]
    twice_rank = down_factor_pool.shape[2]
    rank_size = twice_rank // 2
    share_rows = down_factor_pool.shape[1] // device_shares
    local_count = down_factor_pool.shape[0]
    seg_count = segment_adapters.shape[1]
    narrow = local_hidden_width // groups
    local_down_factor = down_factor_pool.reshape(
        local_count, device_shares, share_rows * twice_rank
    )
    local_up_factor = up_factor_pool.reshape(local_count, device_shares, -1)
    a_spread, b_spread = (
        lax.all_to_all(local_down_factor, ("tp", "cores"), split_axis=1, concat_axis=0, tiled=True),
        lax.all_to_all(local_up_factor, ("tp", "cores"), split_axis=1, concat_axis=0, tiled=True),
    )
    all_slots = jnp.take(adapter_pool_rows, segment_adapters)
    a_wanted = jnp.take(a_spread, all_slots, axis=0)
    b_wanted = jnp.take(b_spread, all_slots, axis=0)
    a_arrived, b_arrived = (
        lax.all_to_all(a_wanted, "grp", split_axis=0, concat_axis=2, tiled=True),
        lax.all_to_all(b_wanted, "grp", split_axis=0, concat_axis=2, tiled=True),
    )
    a_chosen = a_arrived.reshape(seg_count, groups, -1)
    b_chosen = b_arrived.reshape(seg_count, groups, -1)
    gathered = lax.all_gather(tokens, ("tp", "cores"), axis=1, tiled=True)
    frozen_output = jnp.dot(
        gathered,
        gate_up_weight.reshape(full_width, 2 * local_hidden_width),
        preferred_element_type=jnp.float32,
    )
    frozen_output = frozen_output.reshape(token_count, 2, local_hidden_width)
    tile_count = token_count // TILE
    tile_seg = tile_segments(segment_tile_counts[0], tile_count)
    a_tiles = jnp.take(a_chosen, tile_seg, axis=0).reshape(
        tile_count, groups * share_rows, twice_rank
    )
    own_features = lax.dynamic_slice_in_dim(
        gathered.reshape(token_count, groups, device_shares, share_rows), piece_index, 1, axis=2
    )
    own_features = own_features.reshape(tile_count, TILE, groups * share_rows)
    partial_shrink = jnp.einsum(
        "tkd,tdr->tkr", own_features, a_tiles, preferred_element_type=jnp.float32
    )
    reduced_input = lax.psum(partial_shrink, ("tp", "cores")).astype(jnp.bfloat16)
    b_tiles = jnp.take(b_chosen, tile_seg, axis=0).reshape(tile_count, groups, rank_size, 2, narrow)
    gate_adapter_delta = jnp.einsum(
        "tkr,tmrw->tkmw",
        reduced_input[:, :, :rank_size],
        b_tiles[:, :, :, 0, :],
        preferred_element_type=jnp.float32,
    )
    up_adapter_delta = jnp.einsum(
        "tkr,tmrw->tkmw",
        reduced_input[:, :, rank_size:],
        b_tiles[:, :, :, 1, :],
        preferred_element_type=jnp.float32,
    )
    gate_combined = frozen_output[:, 0, :] + adapter_scale * gate_adapter_delta.reshape(
        token_count, local_hidden_width
    )
    up_combined = frozen_output[:, 1, :] + adapter_scale * up_adapter_delta.reshape(
        token_count, local_hidden_width
    )
    return (jax.nn.silu(gate_combined) * up_combined).astype(jnp.bfloat16)


def solution(mesh):
    return jax.shard_map(
        per_device,
        mesh=mesh,
        in_specs=(
            P("grp", ("tp", "cores")),
            P(None, None, ("tp", "cores")),
            P(("tp", "cores"), "grp", None),
            P(("tp", "cores"), "grp", None, None, None),
            P(),
            P("grp", None),
            P(),
        ),
        out_specs=P("grp", ("tp", "cores")),
        check_vma=False,
    )
```

profile of v0, /device:TPU:0, one launch (start us, length us, event | category | flops | bytes accessed | tf_op | source)
XLA Modules:
  0.0 634.1 jit_solution(12954752661760870075)
XLA Ops:
  6.5 4.0 reshape.199
  11.1 7.3 %reduce.3 = bf16[8,65536]{1,0:T(8,128)(2,1)S(1)} reduce(bf16[8,1,65536]{2,1,0:T(2,128)(2,1)S(1)} %bitcast.106, bf16[]{:T(256)} %broadcast.154), dimensions={1}, to_apply=%bitcast.85.reduce_sub_computation | reduce | bytes 2097154
  18.4 1.9 reshape.206
  20.3 7.5 %all-to-all-start = ((bf16[8,2,32768]{2,1,0:T(2,128)(2,1)}), bf16[8,2,32768]{2,1,0:T(2,128)(2,1)S(1)}, u32[]{:S(2)}, u32[]{:S(2)}) async-start(bf16[8,2,32768]{2,1,0:T(2,128)(2,1)} %reshape.206), calls=%async_computation | async-start | bytes 2097152 | tf_op jit(solution)/shard_map/all_to_all | solution.py:42
  28.8 4.1 reshape.200
  32.9 13.0 %reduce.2 = bf16[8,131072]{1,0:T(8,128)(2,1)S(1)} reduce(bf16[8,1,131072]{2,1,0:T(2,128)(2,1)} %bitcast.100, bf16[]{:T(256)} %broadcast.154), dimensions={1}, to_apply=%bitcast.83.reduce_sub_computation | reduce | bytes 4194306
  45.9 3.2 reshape.204
  49.1 4.4 all-to-all-done
  54.5 3.6 all-to-all-start.2
  58.1 5.8 reshape.207
  63.9 2.7 copy.81
  66.6 3.0 gather_fusion.1
  69.6 4.2 reshape.131
  73.8 3.9 select_bitcast_fusion
  77.6 28.9 %all-to-all-done.2 = bf16[8,2,65536]{2,1,0:T(2,128)(2,1)S(1)} async-done(((bf16[8,2,65536]{2,1,0:T(2,128)(2,1)}), bf16[8,2,65536]{2,1,0:T(2,128)(2,1)S(1)}, u32[]{:S(2)}, u32[]{:S(2)}) %all-to-all-start.2) | async-done | bytes 2097184 | tf_op jit(solution)/shard_map/all_to_all | solution.py:43
  106.5 4.7 all-to-all-start.1
  111.2 4.3 reshape.205
  115.5 4.5 copy.79
  120.2 3.0 gather_fusion.3
  123.1 4.2 reshape.149
  128.9 2.6 reshape.159
  131.6 5.8 fusion.8
  137.3 5.0 all-to-all-start.3
  143.2 45.1 %copy.69 = bf16[1024,8,2,2048]{3,1,2,0:T(8,128)(2,1)} copy(bf16[1024,8,2,2048]{3,2,1,0:T(2,128)(2,1)} %bitcast.33) | data formatting | bytes 134217728
  188.3 83.4 %copy.48 = bf16[4096,8192]{1,0:T(8,128)(2,1)} copy(bf16[4096,8192]{0,1:T(8,128)(2,1)} %bitcast.1) | data formatting | bytes 134217728 | tf_op jit(solution)/shard_map/dot_general | solution.py:55
  271.8 3.1 copy.80
  274.9 5.4 gather_fusion.2
  280.3 7.9 %gather.27 = bf16[8,1024,256]{2,1,0:T(8,128)(2,1)} reshape(bf16[8,4,65536]{2,1,0:T(4,128)(2,1)} %gather_fusion.2) | data formatting | bytes 8388608 | tf_op jit(solution)/shard_map/jit(_take)/gather | solution.py:63
  288.3 5.2 copy.78
  294.5 5.4 gather_fusion.5
  299.9 5.5 gather_fusion.6
  305.4 8.3 %pad_maximum_fusion = bf16[8,4,131072]{2,1,0:T(4,128)(2,1)} fusion(bf16[8,4,65536]{2,1,0:T(4,128)(2,1)} %gather_fusion.6, bf16[8,4,65536]{2,1,0:T(4,128)(2,1)} %gather_fusion.5), kind=kLoop, calls=%fused_computation.15 | loop fusion | flops 16777216 | bytes 16777216
  313.8 12.5 %reshape.201 = bf16[8,4,128,2,512]{4,3,2,1,0:T(2,128)(2,1)} reshape(bf16[8,4,131072]{2,1,0:T(4,128)(2,1)} %pad_maximum_fusion) | data formatting | bytes 16777216 | tf_op jit(solution)/shard_map/jit(_take)/gather | solution.py:74
  326.3 8.2 %copy_select_fusion = bf16[8,4,128,2,512]{4,2,1,0,3:T(8,128)(2,1)} fusion(bf16[8,4,128,2,512]{4,3,2,1,0:T(2,128)(2,1)} %reshape.201, pred[8]{0:T(512)(128)(4,1)S(1)} %compare_and_fusion.1), kind=kLoop, calls=%fused_computation.16 | loop fusion | flops 4194304 | bytes 16777224 | tf_op jit(solution)/shard_map/jit(_take)/select_n | solution.py:74
  334.6 37.6 %all-gather.2.cloned.1.call-done = bf16[1024,8192]{1,0:T(8,128)(2,1)} async-done(((bf16[1024,1024]{1,0:T(8,128)(2,1)}), bf16[1024,8192]{1,0:T(8,128)(2,1)}) %all-gather.2.cloned.1.call-update) | async-done | bytes 16777232 | tf_op jit(solution)/shard_map/all_gather | solution.py:54
  372.2 10.3 %copy.70 = bf16[128,8,32,256]{3,2,1,0:T(8,128)(2,1)S(1)} copy(bf16[128,8,32,256]{3,1,2,0:T(8,128)(2,1)} %bitcast.102) | data formatting | bytes 33554432
  382.4 13.7 %dynamic-slice_reduce_fusion = bf16[1024,4,256]{2,1,0:T(4,128)(2,1)S(1)} fusion(bf16[1024,4,8,256]{3,2,1,0:T(8,128)(2,1)S(1)} %bitcast.98, s32[]{:T(128)S(6)} %select_n.80), kind=kLoop, calls=%fused_computation.27 | loop fusion | bytes 4194308 | tf_op jit(solution)/shard_map/dynamic_slice | solution.py:66
  396.1 2.7 reshape.202
  398.8 3.8 fusion.9
  402.6 70.0 %all-reduce.1 = bf16[8,128,256]{2,1,0:T(8,128)(2,1)S(1)} all-reduce(f32[8,128,256]{2,1,0:T(8,128)S(1)} %fusion.9), channel_id=1, replica_groups=mesh['grp'=4,'tp'=4,'cores'=2] {'tp','cores'}, use_global_device_ids=true, to_apply=%region_2.3 | all-reduce | flops 262144 | bytes 1572864 | tf_op jit(solution)/shard_map/psum | solution.py:73
  472.6 6.6 %broadcast_multiply_fusion.1 = f32[8,128,4,512]{3,1,2,0:T(8,128)} fusion(bf16[8,4,128,2,512]{4,2,1,0,3:T(8,128)(2,1)} %copy_select_fusion, bf16[8,128,256]{2,1,0:T(8,128)(2,1)S(1)} %all-reduce.1), kind=kOutput, calls=%fused_computation.24 | convolution fusion | flops 538968064 | bytes 12845056 | tf_op jit(solution)/shard_map/tkr,tmrw->tkmw/dot_general | solution.py:75
  479.2 6.6 %broadcast_multiply_fusion = f32[8,128,4,512]{3,1,2,0:T(8,128)} fusion(bf16[8,4,128,2,512]{4,2,1,0,3:T(8,128)(2,1)} %copy_select_fusion, bf16[8,128,256]{2,1,0:T(8,128)(2,1)S(1)} %all-reduce.1), kind=kOutput, calls=%fused_computation.23 | convolution fusion | flops 538968064 | bytes 12845056 | tf_op jit(solution)/shard_map/tkr,tmrw->tkmw/dot_general | solution.py:81
  485.8 12.1 %copy.60 = f32[8,128,4,512]{3,2,1,0:T(4,128)} copy(f32[8,128,4,512]{3,1,2,0:T(8,128)} %broadcast_multiply_fusion) | data formatting | bytes 16777216 | tf_op jit(solution)/shard_map/mul | solution.py:90
  497.9 11.1 %copy.72 = f32[128,8,4,512]{3,1,2,0:T(8,128)} copy(f32[128,8,4,512]{3,2,1,0:T(4,128)} %bitcast.94) | data formatting | bytes 16777216
  509.0 12.1 %copy.59 = f32[8,128,4,512]{3,2,1,0:T(4,128)} copy(f32[8,128,4,512]{3,1,2,0:T(8,128)} %broadcast_multiply_fusion.1) | data formatting | bytes 16777216 | tf_op jit(solution)/shard_map/mul | solution.py:87
  521.0 10.8 %copy.71 = f32[128,8,4,512]{3,1,2,0:T(8,128)} copy(f32[128,8,4,512]{3,2,1,0:T(4,128)} %bitcast.95) | data formatting | bytes 16777216
  531.8 80.5 %fusion = f32[1024,2,2048]{2,0,1:T(8,128)} fusion(bf16[2,2048,8192]{2,1,0:T(8,128)(2,1)} %bitcast.2, bf16[1024,8192]{1,0:T(8,128)(2,1)} %all-gather.2.cloned.1.call-done), kind=kOutput, calls=%fused_computation.7 | convolution fusion | flops 68719476736 | bytes 100663296 | tf_op jit(solution)/shard_map/dot_general | solution.py:55
  612.3 14.8 %fusion.4 = bf16[1024,2048]{1,0:T(8,128)(2,1)} fusion(f32[1024,2048]{1,0:T(8,128)} %bitcast.96, f32[1024,2,2048]{2,0,1:T(8,128)} %fusion, f32[1024,2048]{1,0:T(8,128)} %bitcast.97), kind=kLoop, calls=%fused_computation.12 | loop fusion | flops 16777216 | bytes 37748736 | tf_op jit(solution)/shard_map/convert_element_type | solution.py:93
  (33 shorter events, 6.4 us)
Async XLA Ops:
  6.5 21.4 %copy-start = (s32[8]{0:T(128)S(1)}, s32[8]{0:T(128)}, u32[]{:S(2)}) copy-start(s32[8]{0:T(128)} %param.13) | copy-start | bytes 100
  10.5 17.3 %copy-start.4 = (s32[4,3]{1,0:T(4,128)S(1)}, s32[4,3]{1,0:T(4,128)}, u32[]{:S(2)}) copy-start(s32[4,3]{1,0:T(4,128)} %param.11) | copy-start | bytes 148
  18.4 10.4 %copy-start.3 = (bf16[1,1,8,128,1024]{4,3,2,1,0:T(8,128)(2,1)S(1)}, bf16[1,1,8,128,1024]{4,3,2,1,0:T(8,128)(2,1)}, u32[]{:S(2)}) copy-start(bf16[1,1,8,128,1024]{4,3,2,1,0:T(8,128)(2,1)} %param.10) | copy-start | bytes 6291460
  20.3 33.2 %all-to-all-start = ((bf16[8,2,32768]{2,1,0:T(2,128)(2,1)}), bf16[8,2,32768]{2,1,0:T(2,128)(2,1)S(1)}, u32[]{:S(2)}, u32[]{:S(2)}) async-start(bf16[8,2,32768]{2,1,0:T(2,128)(2,1)} %reshape.206), calls=%async_computation | async-start | bytes 2097152 | tf_op jit(solution)/shard_map/all_to_all | solution.py:42
  53.5 1.0 copy-start.2
  54.5 52.0 %all-to-all-start.2 = ((bf16[8,2,65536]{2,1,0:T(2,128)(2,1)}), bf16[8,2,65536]{2,1,0:T(2,128)(2,1)S(1)}, u32[]{:S(2)}, u32[]{:S(2)}) async-start(bf16[8,2,65536]{2,1,0:T(2,128)(2,1)} %reshape.204), calls=%async_computation.2 | async-start | bytes 4194304 | tf_op jit(solution)/shard_map/all_to_all | solution.py:43
  106.5 30.8 %all-to-all-start.1 = ((bf16[4,3,1,65536]{3,1,2,0:T(4,128)(2,1)}), bf16[4,3,1,65536]{3,1,2,0:T(4,128)(2,1)}, u32[]{:S(2)}, u32[]{:S(2)}) async-start(bf16[4,3,1,65536]{3,1,2,0:T(4,128)(2,1)} %select_bitcast_fusion), calls=%async_computation.1 | async-start | bytes 4194304 | tf_op jit(solution)/shard_map/all_to_all | solution.py:49
  137.3 5.7 copy-start.5
  137.3 150.9 %all-to-all-start.3 = ((bf16[4,3,1,131072]{3,1,2,0:T(4,128)(2,1)}), bf16[4,3,1,131072]{3,1,2,0:T(4,128)(2,1)}, u32[]{:S(2)}, u32[]{:S(2)}) async-start(bf16[4,3,1,131072]{3,1,2,0:T(4,128)(2,1)} %fusion.8), calls=%async_computation.3 | async-start | bytes 8388608 | tf_op jit(solution)/shard_map/all_to_all | solution.py:50
  142.3 229.8 %all-gather.2.cloned.1.call-start = ((), (), s32[]{:S(2)}) async-start(), calls=%async_computation.4 | async-start | bytes 18874368 | tf_op jit(solution)/shard_map/all_gather | solution.py:54
  612.3 14.8 %copy-start.1 = (s32[8]{0:T(128)S(1)}, s32[8]{0:T(128)}, u32[]{:S(2)}) copy-start(s32[8]{0:T(128)} %param.13) | copy-start | bytes 100
Sparse Core Ops, SparseCore 0:
  145.3 226.8 all-gather.1
where the time goes:
time: 644 us; the launch traced here: 634 us
  local copies, waits for them, and re-layouts  299 us (46%)
  matrix products  97.5 us (15%)
  waiting for transfers between devices  71.2 us (11%)
  blocking collectives  70 us (11%)
  other arithmetic  61.6 us (10%)
  starting transfers between devices  21.2 us (3%)
  between operations  13.8 us (2%)
    unnamed x23, local copies, waits for them, and re-layouts  101 us
    dot_general x1, local copies, waits for them, and re-layouts, per_device(): jnp.dot(gathered, gate_up_weight.reshape(full_width, 2 * local_hidden_wid...  83.4 us
    dot_general x1, matrix products, per_device(): jnp.dot(gathered, gate_up_weight.reshape(full_width, 2 * local_hidden_wid...  80.5 us
    psum x1, blocking collectives, per_device(): lax.psum(partial_shrink, ('tp', 'cores')).astype(jnp.bfloat16)  70 us
    all_gather x1, waiting for transfers between devices, per_device(): gathered = lax.all_gather(tokens, ('tp', 'cores'), axis=1, tiled=True)  37.6 us
    all_to_all x1, waiting for transfers between devices, per_device(): lax.all_to_all(local_up_factor, ('tp', 'cores'), split_axis=1, concat_axi...  28.9 us
    unnamed x3, other arithmetic  28.6 us
    gather x4, local copies, waits for them, and re-layouts, per_device(): jnp.take(b_chosen, tile_seg, axis=0)  24.6 us
  transfers between devices with their start and end apart: 5, of which 3 were waited for; matrix products, arithmetic and copies ran while one was open for 41% of the time, Pallas kernels for 0%

commit v1 on v0

--- a/solution.py
+++ b/solution.py
@@ -1,3 +1,4 @@
+import functools
 import jax
 import jax.numpy as jnp
 from jax import lax
@@ -5,6 +6,41 @@
 
 TILE = 128
 adapter_scale = 0.5
+
+
+def slabs_fit(view, device_axis):
+    local_now, part_now, block_out = (
+        lax.axis_size(device_axis),
+        lax.axis_index(device_axis),
+        view.shape[1],
+    )
+    pile = []
+    for j0, idx in enumerate(view.shape):
+        pile.append(idx * local_now if j0 == 1 else idx)
+    t_next = lax.dynamic_update_slice_in_dim(
+        jnp.zeros(pile, view.dtype), view, part_now * block_out, axis=1
+    )
+    formed = back = view
+    for at in range(1, local_now // 2 + 1):
+        slots = []
+        for j0 in range(local_now):
+            slots.append((j0, (j0 + 1) % local_now))
+        formed = lax.ppermute(formed, axis_name=device_axis, perm=slots)
+        t_next = lax.dynamic_update_slice_in_dim(
+            t_next, formed, (part_now - at) % local_now * block_out, axis=1
+        )
+        if 2 * at < local_now:
+            in_order = []
+            for j0 in range(local_now):
+                in_order.append((j0, (j0 - 1) % local_now))
+            back = lax.ppermute(back, axis_name=device_axis, perm=in_order)
+            t_next = lax.dynamic_update_slice_in_dim(
+                t_next, back, (part_now + at) % local_now * block_out, axis=1
+            )
+    return t_next
+
+
+sheets_detail = functools.partial(slabs_fit, device_axis=("tp", "cores"))
 
 
 def tile_segments(tile_lengths, tile_count):
@@ -51,7 +87,7 @@
     )
     a_chosen = a_arrived.reshape(seg_count, groups, -1)
     b_chosen = b_arrived.reshape(seg_count, groups, -1)
-    gathered = lax.all_gather(tokens, ("tp", "cores"), axis=1, tiled=True)
+    gathered = sheets_detail(tokens)
     frozen_output = jnp.dot(
         gathered,
         gate_up_weight.reshape(full_width, 2 * local_hidden_width),

time: 644 us -> 794 us (1.23)
  waiting for transfers between devices: 71.2 us -> 151 us
  starting transfers between devices: 21.2 us -> 80.7 us
  local copies, waits for them, and re-layouts: 299 us -> 325 us
  between operations: 13.8 us -> 0.51 us
    ppermute x0 -> x7, waiting for transfers between devices: none -> 102 us  [the longest x4 102 us: slabs_fit(): formed = lax.ppermute(formed, axis_name=device_axis, perm=slots)]
    all_to_all x1, starting transfers between devices: 3.6 us -> 46.2 us  [per_device(): lax.all_to_all(local_up_factor, ('tp', 'cores'), split_axis=1, concat_axi...]
    all_gather x1 -> x0, waiting for transfers between devices: 37.6 us -> none  [per_device(): gathered = lax.all_gather(tokens, ('tp', 'cores'), axis=1, tiled=True)]
    dynamic_update_slice x0 -> x8, local copies, waits for them, and re-layouts: none -> 21.5 us  [the longest x4 10.8 us: slabs_fit(): lax.dynamic_update_slice_in_dim(t_next, formed, (part_now - at) % local_n...]
    all_to_all x1, waiting for transfers between devices: 28.9 us -> 48 us  [per_device(): lax.all_to_all(local_up_factor, ('tp', 'cores'), split_axis=1, concat_axi...]
    ppermute x0 -> x7, starting transfers between devices: none -> 17.4 us  [the longest x3 10.3 us: slabs_fit(): back = lax.ppermute(back, axis_name=device_axis, perm=in_order)]
    unnamed x23 -> x29, local copies, waits for them, and re-layouts: 101 us -> 100 us
    unnamed x3 -> x4, other arithmetic: 28.6 us -> 28.5 us
  transfers between devices with their start and end apart: 5 -> 11, of which waited for: 3 -> 5; matrix products, arithmetic and copies ran while one was open for 41% -> 36% of each run, Pallas kernels for 0% -> 0%
where the time goes in v1:
time: 794 us; the launch traced here: 784 us
  local copies, waits for them, and re-layouts  325 us (41%)
  waiting for transfers between devices  151 us (19%)
  matrix products  97.8 us (12%)
  starting transfers between devices  80.7 us (10%)
  blocking collectives  69.8 us (9%)
  other arithmetic  59 us (7%)
    ppermute x4, waiting for transfers between devices, slabs_fit(): formed = lax.ppermute(formed, axis_name=device_axis, perm=slots)  102 us
    unnamed x29, local copies, waits for them, and re-layouts  100 us
    dot_general x1, local copies, waits for them, and re-layouts, per_device(): jnp.dot(gathered, gate_up_weight.reshape(full_width, 2 * local_hidden_wid...  83.3 us
    dot_general x1, matrix products, per_device(): jnp.dot(gathered, gate_up_weight.reshape(full_width, 2 * local_hidden_wid...  80.7 us
    psum x1, blocking collectives, per_device(): lax.psum(partial_shrink, ('tp', 'cores')).astype(jnp.bfloat16)  69.8 us
    all_to_all x1, waiting for transfers between devices, per_device(): lax.all_to_all(local_up_factor, ('tp', 'cores'), split_axis=1, concat_axi...  48 us
    all_to_all x1, starting transfers between devices, per_device(): lax.all_to_all(local_up_factor, ('tp', 'cores'), split_axis=1, concat_axi...  46.2 us
    unnamed x4, other arithmetic  28.5 us
  transfers between devices with their start and end apart: 11, of which 5 were waited for; matrix products, arithmetic and copies ran while one was open for 36% of the time, Pallas kernels for 0%

profile of v1, /device:TPU:0, one launch (start us, length us, event | category | flops | bytes accessed | tf_op | source)
XLA Modules:
  0.0 783.9 jit_solution(10731022973226848978)
XLA Ops:
  0.0 4.0 reshape.199
  4.5 7.2 reduce.3
  13.6 7.3 all-to-all-start
  26.8 4.1 reshape.200
  30.9 12.9 %reduce.2 = bf16[8,131072]{1,0:T(8,128)(2,1)S(1)} reduce(bf16[8,1,131072]{2,1,0:T(2,128)(2,1)} %bitcast.102, bf16[]{:T(256)} %broadcast.161), dimensions={1}, to_apply=%bitcast.83.reduce_sub_computation | reduce | bytes 4194306
  43.8 3.2 reshape.204
  49.1 46.2 %all-to-all-start.2 = ((bf16[8,2,65536]{2,1,0:T(2,128)(2,1)}), bf16[8,2,65536]{2,1,0:T(2,128)(2,1)S(1)}, u32[]{:S(2)}, u32[]{:S(2)}) async-start(bf16[8,2,65536]{2,1,0:T(2,128)(2,1)} %reshape.204), calls=%async_computation.2 | async-start | bytes 4194304 | tf_op jit(solution)/shard_map/all_to_all | solution.py:79
  95.3 5.8 reshape.207
  106.8 4.2 reshape.131
  111.0 3.9 select_bitcast_fusion
  114.9 25.4 %collective-permute-done = bf16[1024,1024]{1,0:T(8,128)(2,1)} collective-permute-done((bf16[1024,1024]{1,0:T(8,128)(2,1)}, bf16[1024,1024]{1,0:T(8,128)(2,1)}, u32[]{:S(2)}, u32[]{:S(2)}) %collective-permute-start) | collective-permute-done | bytes 2097184 | tf_op jit(solution)/shard_map/ppermute | solution.py:28
  145.0 48.0 %all-to-all-done.2 = bf16[8,2,65536]{2,1,0:T(2,128)(2,1)S(1)} async-done(((bf16[8,2,65536]{2,1,0:T(2,128)(2,1)}), bf16[8,2,65536]{2,1,0:T(2,128)(2,1)S(1)}, u32[]{:S(2)}, u32[]{:S(2)}) %all-to-all-start.2) | async-done | bytes 2097184 | tf_op jit(solution)/shard_map/all_to_all | solution.py:79
  193.0 4.7 all-to-all-start.1
  197.7 4.3 reshape.205
  202.0 4.5 copy.75
  209.6 4.2 reshape.149
  218.0 5.8 fusion.8
  223.8 5.1 all-to-all-start.3
  229.0 44.2 %copy.65 = bf16[1024,8,2,2048]{3,1,2,0:T(8,128)(2,1)} copy(bf16[1024,8,2,2048]{3,2,1,0:T(2,128)(2,1)} %bitcast.33) | data formatting | bytes 134217728
  273.3 83.3 %copy.46 = bf16[4096,8192]{1,0:T(8,128)(2,1)} copy(bf16[4096,8192]{0,1:T(8,128)(2,1)} %bitcast.1) | data formatting | bytes 134217728 | tf_op jit(solution)/shard_map/dot_general | solution.py:91
  356.9 6.0 broadcast_in_dim.49
  367.5 3.1 constant_dynamic-update-slice_fusion.5
  370.5 3.1 copy.76
  373.6 5.4 gather_fusion.2
  379.0 7.9 %gather.27 = bf16[8,1024,256]{2,1,0:T(8,128)(2,1)} reshape(bf16[8,4,65536]{2,1,0:T(4,128)(2,1)} %gather_fusion.2) | data formatting | bytes 8388608 | tf_op jit(solution)/shard_map/jit(_take)/gather | solution.py:99
  386.9 5.2 collective-permute-start.5
  398.2 5.2 copy.74
  404.5 5.4 gather_fusion.5
  409.9 5.4 gather_fusion.6
  415.3 62.8 %collective-permute-done.4 = bf16[1024,1024]{1,0:T(8,128)(2,1)} collective-permute-done((bf16[1024,1024]{1,0:T(8,128)(2,1)}, bf16[1024,1024]{1,0:T(8,128)(2,1)}, u32[]{:S(2)}, u32[]{:S(2)}) %collective-permute-start.4) | collective-permute-done | bytes 2097184 | tf_op jit(solution)/shard_map/ppermute | solution.py:28
  480.6 8.4 %pad_maximum_fusion = bf16[8,4,131072]{2,1,0:T(4,128)(2,1)} fusion(bf16[8,4,65536]{2,1,0:T(4,128)(2,1)} %gather_fusion.6, bf16[8,4,65536]{2,1,0:T(4,128)(2,1)} %gather_fusion.5), kind=kLoop, calls=%fused_computation.15 | loop fusion | flops 16777216 | bytes 16777216
  489.0 12.6 %reshape.201 = bf16[8,4,128,2,512]{4,3,2,1,0:T(2,128)(2,1)} reshape(bf16[8,4,131072]{2,1,0:T(4,128)(2,1)} %pad_maximum_fusion) | data formatting | bytes 16777216 | tf_op jit(solution)/shard_map/jit(_take)/gather | solution.py:110
  501.6 8.0 %copy_select_fusion = bf16[8,4,128,2,512]{4,2,1,0,3:T(8,128)(2,1)} fusion(bf16[8,4,128,2,512]{4,3,2,1,0:T(2,128)(2,1)} %reshape.201, pred[8]{0:T(512)(128)(4,1)S(1)} %compare_and_fusion.1), kind=kLoop, calls=%fused_computation.16 | loop fusion | flops 4194304 | bytes 16777224 | tf_op jit(solution)/shard_map/jit(_take)/select_n | solution.py:110
  509.6 3.1 constant_dynamic-update-slice_fusion.2
  512.7 3.1 constant_dynamic-update-slice_fusion.1
  515.8 13.6 %collective-permute-done.6 = bf16[1024,1024]{1,0:T(8,128)(2,1)S(1)} collective-permute-done((bf16[1024,1024]{1,0:T(8,128)(2,1)}, bf16[1024,1024]{1,0:T(8,128)(2,1)S(1)}, u32[]{:S(2)}, u32[]{:S(2)}) %collective-permute-start.6) | collective-permute-done | bytes 2097184 | tf_op jit(solution)/shard_map/ppermute | solution.py:28
  531.0 10.3 %copy.66 = bf16[128,8,32,256]{3,2,1,0:T(8,128)(2,1)S(1)} copy(bf16[128,8,32,256]{3,1,2,0:T(8,128)(2,1)} %bitcast.35) | data formatting | bytes 33554432
  541.2 13.7 %dynamic-slice_reduce_fusion = bf16[1024,4,256]{2,1,0:T(4,128)(2,1)S(1)} fusion(bf16[1024,4,8,256]{3,2,1,0:T(8,128)(2,1)S(1)} %bitcast.100, s32[]{:T(128)S(6)} %select_n.150), kind=kLoop, calls=%fused_computation.27 | loop fusion | bytes 4194308 | tf_op jit(solution)/shard_map/dynamic_slice | solution.py:102
  557.6 3.8 fusion.9
  561.4 69.8 %all-reduce.1 = bf16[8,128,256]{2,1,0:T(8,128)(2,1)S(1)} all-reduce(f32[8,128,256]{2,1,0:T(8,128)S(1)} %fusion.9), channel_id=1, replica_groups=mesh['grp'=4,'tp'=4,'cores'=2] {'tp','cores'}, use_global_device_ids=true, to_apply=%region_2.3 | all-reduce | flops 262144 | bytes 1572864 | tf_op jit(solution)/shard_map/psum | solution.py:109
  631.2 6.6 broadcast_multiply_fusion.1
  637.8 6.7 broadcast_multiply_fusion
  644.6 80.7 %fusion = f32[1024,2,2048]{2,0,1:T(8,128)} fusion(bf16[2,2048,8192]{2,1,0:T(8,128)(2,1)} %bitcast.2, bf16[1024,8192]{1,0:T(8,128)(2,1)} %constant_dynamic-update-slice_fusion), kind=kOutput, calls=%fused_computation.7 | convolution fusion | flops 68719476736 | bytes 100663296 | tf_op jit(solution)/shard_map/dot_general | solution.py:91
  725.3 12.1 %copy.56 = f32[8,128,4,512]{3,2,1,0:T(4,128)} copy(f32[8,128,4,512]{3,1,2,0:T(8,128)} %broadcast_multiply_fusion.1) | data formatting | bytes 16777216 | tf_op jit(solution)/shard_map/mul | solution.py:123
  737.4 10.7 %copy.67 = f32[128,8,4,512]{3,1,2,0:T(8,128)} copy(f32[128,8,4,512]{3,2,1,0:T(4,128)} %bitcast.94) | data formatting | bytes 16777216
  748.1 12.2 %copy.57 = f32[8,128,4,512]{3,2,1,0:T(4,128)} copy(f32[8,128,4,512]{3,1,2,0:T(8,128)} %broadcast_multiply_fusion) | data formatting | bytes 16777216 | tf_op jit(solution)/shard_map/mul | solution.py:126
  760.3 10.9 %copy.68 = f32[128,8,4,512]{3,1,2,0:T(8,128)} copy(f32[128,8,4,512]{3,2,1,0:T(4,128)} %bitcast.95) | data formatting | bytes 16777216
  771.3 12.5 %fusion.4 = bf16[1024,2048]{1,0:T(8,128)(2,1)} fusion(f32[1024,2048]{1,0:T(8,128)} %bitcast.99, f32[1024,2,2048]{2,0,1:T(8,128)} %fusion, f32[1024,2048]{1,0:T(8,128)S(1)} %bitcast.98), kind=kLoop, calls=%fused_computation.12 | loop fusion | flops 16777216 | bytes 37748736 | tf_op jit(solution)/shard_map/convert_element_type | solution.py:129
  (60 shorter events, 47.0 us)
Async XLA Ops:
  0.0 25.9 %copy-start = (s32[8]{0:T(128)S(1)}, s32[8]{0:T(128)}, u32[]{:S(2)}) copy-start(s32[8]{0:T(128)} %param.13) | copy-start | bytes 100
  4.0 21.8 %copy-start.5 = (s32[4,3]{1,0:T(4,128)S(1)}, s32[4,3]{1,0:T(4,128)}, u32[]{:S(2)}) copy-start(s32[4,3]{1,0:T(4,128)} %param.11) | copy-start | bytes 148
  11.7 15.0 %copy-start.3 = (bf16[1,1,8,128,1024]{4,3,2,1,0:T(8,128)(2,1)S(1)}, bf16[1,1,8,128,1024]{4,3,2,1,0:T(8,128)(2,1)}, u32[]{:S(2)}) copy-start(bf16[1,1,8,128,1024]{4,3,2,1,0:T(8,128)(2,1)} %param.10) | copy-start | bytes 6291460
  13.6 34.5 %all-to-all-start = ((bf16[8,2,32768]{2,1,0:T(2,128)(2,1)}), bf16[8,2,32768]{2,1,0:T(2,128)(2,1)S(1)}, u32[]{:S(2)}, u32[]{:S(2)}) async-start(bf16[8,2,32768]{2,1,0:T(2,128)(2,1)} %reshape.206), calls=%async_computation | async-start | bytes 2097152 | tf_op jit(solution)/shard_map/all_to_all | solution.py:78
  20.9 119.4 %collective-permute-start = (bf16[1024,1024]{1,0:T(8,128)(2,1)}, bf16[1024,1024]{1,0:T(8,128)(2,1)}, u32[]{:S(2)}, u32[]{:S(2)}) collective-permute-start(bf16[1024,1024]{1,0:T(8,128)(2,1)} %param.7), channel_id=1, source_target_pairs={{0,1},{1,2},{2,3},{3,4},{4,5},{5,6},{6,7},{7,0},{8,9},{9,10},{10,1... | collective-permute-start | bytes 6291464 | tf_op jit(solution)/shard_map/ppermute | solution.py:28
  22.9 119.8 %collective-permute-start.1 = (bf16[1024,1024]{1,0:T(8,128)(2,1)}, bf16[1024,1024]{1,0:T(8,128)(2,1)}, u32[]{:S(2)}, u32[]{:S(2)}) collective-permute-start(bf16[1024,1024]{1,0:T(8,128)(2,1)} %param.7), channel_id=1, source_target_pairs={{0,7},{1,0},{2,1},{3,2},{4,3},{5,4},{6,5},{7,6},{8,15},{9,8},{10,9... | collective-permute-start | bytes 6291464 | tf_op jit(solution)/shard_map/ppermute | solution.py:36
  48.1 1.0 copy-start.2
  49.1 143.9 %all-to-all-start.2 = ((bf16[8,2,65536]{2,1,0:T(2,128)(2,1)}), bf16[8,2,65536]{2,1,0:T(2,128)(2,1)S(1)}, u32[]{:S(2)}, u32[]{:S(2)}) async-start(bf16[8,2,65536]{2,1,0:T(2,128)(2,1)} %reshape.204), calls=%async_computation.2 | async-start | bytes 4194304 | tf_op jit(solution)/shard_map/all_to_all | solution.py:79
  140.3 246.6 %collective-permute-start.2 = (bf16[1024,1024]{1,0:T(8,128)(2,1)}, bf16[1024,1024]{1,0:T(8,128)(2,1)}, u32[]{:S(2)}, u32[]{:S(2)}) collective-permute-start(bf16[1024,1024]{1,0:T(8,128)(2,1)} %collective-permute-done), channel_id=1, source_target_pairs={{0,1},{1,2},{2,3},{3,4},{4,5},{5,6},{6,7},{7,0},{8,9},{9,10},{10,1... | collective-permute-start | bytes 6291464 | tf_op jit(solution)/shard_map/ppermute | solution.py:28
  142.8 244.2 %collective-permute-start.3 = (bf16[1024,1024]{1,0:T(8,128)(2,1)}, bf16[1024,1024]{1,0:T(8,128)(2,1)}, u32[]{:S(2)}, u32[]{:S(2)}) collective-permute-start(bf16[1024,1024]{1,0:T(8,128)(2,1)} %collective-permute-done.1), channel_id=1, source_target_pairs={{0,7},{1,0},{2,1},{3,2},{4,3},{5,4},{6,5},{7,6},{8,15},{9,8},{10,9... | collective-permute-start | bytes 6291464 | tf_op jit(solution)/shard_map/ppermute | solution.py:36
  193.0 30.8 %all-to-all-start.1 = ((bf16[4,3,1,65536]{3,1,2,0:T(4,128)(2,1)}), bf16[4,3,1,65536]{3,1,2,0:T(4,128)(2,1)}, u32[]{:S(2)}, u32[]{:S(2)}) async-start(bf16[4,3,1,65536]{3,1,2,0:T(4,128)(2,1)} %select_bitcast_fusion), calls=%async_computation.1 | async-start | bytes 4194304 | tf_op jit(solution)/shard_map/all_to_all | solution.py:85
  223.8 174.4 %all-to-all-start.3 = ((bf16[4,3,1,131072]{3,1,2,0:T(4,128)(2,1)}), bf16[4,3,1,131072]{3,1,2,0:T(4,128)(2,1)}, u32[]{:S(2)}, u32[]{:S(2)}) async-start(bf16[4,3,1,131072]{3,1,2,0:T(4,128)(2,1)} %fusion.8), calls=%async_computation.3 | async-start | bytes 8388608 | tf_op jit(solution)/shard_map/all_to_all | solution.py:86
  273.3 83.3 %copy-start.6 = (s32[1,3]{1,0:T(1,128)S(1)}, s32[1,3]{1,0:T(1,128)}, u32[]{:S(2)}) copy-start(s32[1,3]{1,0:T(1,128)} %param.12) | copy-start | bytes 40
  356.9 6.0 copy-start.4
  386.9 91.1 %collective-permute-start.4 = (bf16[1024,1024]{1,0:T(8,128)(2,1)}, bf16[1024,1024]{1,0:T(8,128)(2,1)}, u32[]{:S(2)}, u32[]{:S(2)}) collective-permute-start(bf16[1024,1024]{1,0:T(8,128)(2,1)} %collective-permute-done.2), channel_id=1, source_target_pairs={{0,1},{1,2},{2,3},{3,4},{4,5},{5,6},{6,7},{7,0},{8,9},{9,10},{10,1... | collective-permute-start | bytes 6291464 | tf_op jit(solution)/shard_map/ppermute | solution.py:28
  386.9 125.8 %collective-permute-start.5 = (bf16[1024,1024]{1,0:T(8,128)(2,1)}, bf16[1024,1024]{1,0:T(8,128)(2,1)}, u32[]{:S(2)}, u32[]{:S(2)}) collective-permute-start(bf16[1024,1024]{1,0:T(8,128)(2,1)} %collective-permute-done.3), channel_id=1, source_target_pairs={{0,7},{1,0},{2,1},{3,2},{4,3},{5,4},{6,5},{7,6},{8,15},{9,8},{10,9... | collective-permute-start | bytes 6291464 | tf_op jit(solution)/shard_map/ppermute | solution.py:36
  478.0 51.4 %collective-permute-start.6 = (bf16[1024,1024]{1,0:T(8,128)(2,1)}, bf16[1024,1024]{1,0:T(8,128)(2,1)S(1)}, u32[]{:S(2)}, u32[]{:S(2)}) collective-permute-start(bf16[1024,1024]{1,0:T(8,128)(2,1)} %collective-permute-done.4), channel_id=1, source_target_pairs={{0,1},{1,2},{2,3},{3,4},{4,5},{5,6},{6,7},{7,0},{8,9},{9,10},{10,1... | collective-permute-start | bytes 6291464 | tf_op jit(solution)/shard_map/ppermute | solution.py:28
  760.3 11.0 %slice-start = ((s8[8388608]{0:T(1024)(128)(4,1)}), s8[4194304]{0:T(1024)(128)(4,1)S(1)}, s32[]{:S(2)}) async-start(s8[8388608]{0:T(1024)(128)(4,1)} %bitcast.96), calls=%async_computation.4 | async-start | bytes 8388608
  760.3 11.0 %slice-start.1 = ((s8[8388608]{0:T(1024)(128)(4,1)}), s8[4194304]{0:T(1024)(128)(4,1)S(1)}, s32[]{:S(2)}) async-start(s8[8388608]{0:T(1024)(128)(4,1)} %bitcast.96), calls=%async_computation.5 | async-start | bytes 8388608
  771.3 12.5 %copy-start.1 = (s32[8]{0:T(128)S(1)}, s32[8]{0:T(128)}, u32[]{:S(2)}) copy-start(s32[8]{0:T(128)} %param.13) | copy-start | bytes 100
